TPU v7x, 32 devices: a whole 2x2x4 slice. The times are simulated.
32 devices in a mesh: grp: 2 (over x), res: 16 (over z, y, core).
Axes of the slice: x: 2, y: 2, z: 4, core: 2. Of those that a mesh axis runs over, the one named last changes fastest.
Arguments:
- stacked_sequence_embedding: bfloat16 [1024, 8192], P(('grp', 'res')), parts along dimension 0, may hold values from -6 to 6
- normalizer_multiplier: float32 [64], replicated, may hold values from 0.1 to 1.9
- normalizer_additive: float32 [64], replicated, may hold values from -2 to 2
- lhs_projected_tensor: bfloat16 [64, 32], replicated, may hold values from -0.75 to 0.75
- rhs_projected_tensor: bfloat16 [64, 32], replicated, may hold values from -0.75 to 0.75
- pairwise_matrix: bfloat16 [1024, 128], replicated, may hold values from -0.359375 to 0.359375
- pairwise_shift: float32 [128], replicated, may hold values from -3 to 3
Outputs:
- pair_update: bfloat16 [256, 128, 128], P(('grp', 'res')), parts along dimension 0
There are 2 independent parts, one for each index of `grp`. A program takes and returns all parts, laid end to end along the dimension named above; an argument that names none is the same for every part. Nothing has to cross between parts.
All inputs are finite; a program needn't handle non-finite values.
Results may differ from a plain program's by a relative error of at most 0.0047.
Values may be sent and summed in bfloat16 or wider, within the bound.
A program may use at most 128 MiB of HBM per device.

v0:
```python
import jax
import jax.numpy as jnp
from jax import lax
from jax.sharding import PartitionSpec as P


def normalize(member_list, normalizer_multiplier, normalizer_additive):
    center = member_list - jnp.mean(member_list, axis=-1, keepdims=True)
    spread = jnp.mean(center * center, axis=-1, keepdims=True)
    return (
        center * lax.rsqrt(spread + 1e-05) * normalizer_multiplier + normalizer_additive
    ).astype(jnp.bfloat16)


def project_both(
    member_list,
    normalizer_multiplier,
    normalizer_additive,
    lhs_projected_tensor,
    rhs_projected_tensor,
    rows,
    residues,
):
    chans = lhs_projected_tensor.shape[0]
    width = lhs_projected_tensor.shape[1]
    normed = normalize(
        member_list.astype(jnp.float32).reshape(rows * residues, chans),
        normalizer_multiplier,
        normalizer_additive,
    )
    left = (
        jnp.dot(normed, lhs_projected_tensor, preferred_element_type=jnp.float32)
        .astype(jnp.bfloat16)
        .reshape(rows, residues * width)
    )
    right = (
        jnp.dot(normed, rhs_projected_tensor, preferred_element_type=jnp.float32)
        .astype(jnp.bfloat16)
        .reshape(rows, residues * width)
    )
    return (left, right)


def pair_block(left, piece, pairwise_matrix, pairwise_shift, width):
    rows = left.shape[0]
    left_count = left.shape[1] // width
    right_count = piece.shape[1] // width
    outer = (
        lax.dot_general(left, piece, (((0,), (0,)), ((), ())), preferred_element_type=jnp.float32)
        / rows
    )
    flat = outer.reshape(left_count, width, right_count, width).transpose(0, 2, 1, 3)
    flat = flat.reshape(left_count * right_count, width * width).astype(jnp.bfloat16)
    mapped = jnp.dot(flat, pairwise_matrix, preferred_element_type=jnp.float32) + pairwise_shift
    return mapped.astype(jnp.bfloat16).reshape(left_count, right_count, pairwise_matrix.shape[1])


def on_device(
    stacked_sequence_embedding,
    normalizer_multiplier,
    normalizer_additive,
    lhs_projected_tensor,
    rhs_projected_tensor,
    pairwise_matrix,
    pairwise_shift,
):
    chans = lhs_projected_tensor.shape[0]
    width = lhs_projected_tensor.shape[1]
    partition_numbers = lax.all_to_all(
        stacked_sequence_embedding, "res", split_axis=1, concat_axis=0, tiled=True
    )
    rows = partition_numbers.shape[0]
    resid = partition_numbers.shape[1] // chans
    left, right = project_both(
        partition_numbers,
        normalizer_multiplier,
        normalizer_additive,
        lhs_projected_tensor,
        rhs_projected_tensor,
        rows,
        resid,
    )
    return pair_block(
        left,
        lax.all_gather(right, "res", axis=1, tiled=True),
        pairwise_matrix,
        pairwise_shift,
        width,
    )


def solution(mesh):
    in_specs = (P(("grp", "res"), None), P(), P(), P(), P(), P(), P())
    out_specs = P(("grp", "res"), None, None)
    return jax.shard_map(
        on_device, mesh=mesh, in_specs=in_specs, out_specs=out_specs, check_vma=False
    )
```

profile of v0, /device:TPU:0, one launch (start us, length us, event | category | flops | bytes accessed | tf_op | source)
XLA Modules:
  0.0 116.2 jit_solution(17071124105977982926)
XLA Ops:
  6.5 0.0 copy-start
  6.5 0.0 all-gather.2.cloned.1.call-start
  6.5 1.1 copy.23
  7.7 21.7 %all_to_all.13 = bf16[32,16,512]{2,0,1:T(8,128)(2,1)S(1)} all-to-all(bf16[32,16,512]{2,0,1:T(8,128)(2,1)S(1)} %bitcast.28), channel_id=1, replica_groups=mesh['grp'=2,'res'=16] {'res'}, dimensions={1} | all-to-all | bytes 1048576 | tf_op jit(solution)/shard_map/all_to_all | solution.py:69
  29.3 0.1 convert_bitcast_fusion
  29.5 0.4 reshape.38
  29.9 0.0 copy-start.3
  29.9 0.0 copy-start.4
  29.9 0.6 reduce_sum.18
  30.5 1.3 %multiply_reduce_fusion = f32[4096]{0:T(1024)S(1)} fusion(f32[4096,64]{1,0:T(8,128)S(1)} %reshape.38, f32[4096]{0:T(1024)S(1)} %broadcast_multiply_fusion), kind=kLoop, calls=%fused_computation.8 | loop fusion | flops 782336 | bytes 1081344 | tf_op jit(solution)/shard_map/reduce_sum | solution.py:9
  31.8 0.0 copy-start.1
  31.8 0.0 copy-done.3
  31.9 0.0 copy-done.4
  31.9 2.3 %add_convert_fusion = bf16[4096,64]{1,0:T(8,128)(2,1)S(1)} fusion(f32[4096,64]{1,0:T(8,128)S(1)} %reshape.38, f32[64]{0:T(128)S(1)} %copy-done.3, f32[64]{0:T(128)S(1)} %copy-done.4, f32[4096]{0:T(1024)S(1)} %add_rsqrt_fusion, f32[4096]{0:T(1024)S(1)} %broadcast_multiply_fusion), kind=kLoop, calls=%fused_computation.7 | loop fusion | flops 1310720 | bytes 1606144 | tf_op jit(solution)/shard_map/convert_element_type | solution.py:12
  34.2 0.0 copy-done.1
  34.2 0.0 copy-start.2
  34.2 0.4 convolution_convert_fusion
  34.6 0.5 copy.10
  35.1 1.4 %reshape.36 = bf16[512,256]{1,0:T(8,128)(2,1)} reshape(bf16[4096,32]{1,0:T(8,128)(2,1)S(1)} %copy.10) | data formatting | bytes 524288 | tf_op jit(solution)/shard_map/reshape | solution.py:39
  36.6 0.0 all-gather.2.cloned.1.call-update
  36.6 0.0 copy-done.2
  36.6 0.4 convolution_convert_fusion.1
  37.1 0.5 copy.9
  37.6 0.7 reshape.35
  38.3 51.1 %all-gather.2.cloned.1.call-done = bf16[512,4096]{1,0:T(8,128)(2,1)} async-done(((bf16[512,256]{1,0:T(8,128)(2,1)}), bf16[512,4096]{1,0:T(8,128)(2,1)}) %all-gather.2.cloned.1.call-update) | async-done | bytes 4194320 | tf_op jit(solution)/shard_map/all_gather | solution.py:85
  89.4 3.5 %fusion = bf16[256,4096]{1,0:T(8,128)(2,1)S(1)} fusion(bf16[512,256]{1,0:T(8,128)(2,1)S(1)} %reshape.35, bf16[512,4096]{1,0:T(8,128)(2,1)} %all-gather.2.cloned.1.call-done), kind=kOutput, calls=%fused_computation.1 | convolution fusion | flops 1075838976 | bytes 6553600 | tf_op jit(solution)/shard_map/dot_general | solution.py:49
  92.9 8.0 %convert_element_type.41 = bf16[8,32,128,32]{3,2,1,0:T(8,128)(2,1)} reshape(bf16[256,4096]{1,0:T(8,128)(2,1)S(1)} %fusion) | data formatting | bytes 4194304 | tf_op jit(solution)/shard_map/convert_element_type | solution.py:53
  100.9 0.0 copy-start.5
  100.9 7.0 %copy.11 = bf16[8,128,32,32]{1,0,3,2:T(8,128)(2,1)S(1)} copy(bf16[8,128,32,32]{3,1,2,0:T(8,128)(2,1)} %bitcast.26) | data formatting | bytes 4194304 | tf_op jit(solution)/shard_map/convert_element_type | solution.py:53
  107.9 0.0 copy-done
  107.9 0.0 copy-done.5
  107.9 1.5 %fusion.7 = bf16[1024,128]{1,0:T(8,128)(2,1)} fusion(bf16[1024,128]{1,0:T(8,128)(2,1)S(1)} %copy-done, bf16[128,8,8,128]{3,2,1,0:T(8,128)(2,1)S(1)} %bitcast.27, f32[128]{0:T(128)S(1)} %copy-done.5), kind=kOutput, calls=%fused_computation.10 | convolution fusion | flops 268697600 | bytes 2621952 | tf_op jit(solution)/shard_map/dot_general | solution.py:54
  (2 shorter events, 0.0 us)
Async XLA Ops:
  6.5 101.3 %copy-start = (bf16[1024,128]{1,0:T(8,128)(2,1)S(1)}, bf16[1024,128]{1,0:T(8,128)(2,1)}, u32[]{:S(2)}) copy-start(bf16[1024,128]{1,0:T(8,128)(2,1)} %param.12) | copy-start | bytes 786436
  6.5 82.8 %all-gather.2.cloned.1.call-start = ((), (), s32[]{:S(2)}) async-start(), calls=%async_computation.1 | async-start | bytes 4456448 | tf_op jit(solution)/shard_map/all_gather | solution.py:85
  29.9 2.0 %copy-start.3 = (f32[64]{0:T(128)S(1)}, f32[64]{0:T(128)}, u32[]{:S(2)}) copy-start(f32[64]{0:T(128)} %param.9) | copy-start | bytes 772
  29.9 2.0 %copy-start.4 = (f32[64]{0:T(128)S(1)}, f32[64]{0:T(128)}, u32[]{:S(2)}) copy-start(f32[64]{0:T(128)} %param.8) | copy-start | bytes 772
  31.8 2.4 %copy-start.1 = (bf16[64,32]{0,1:T(8,128)(2,1)S(1)}, bf16[64,32]{0,1:T(8,128)(2,1)}, u32[]{:S(2)}) copy-start(bf16[64,32]{0,1:T(8,128)(2,1)} %param.11) | copy-start | bytes 12292
  34.2 2.4 %copy-start.2 = (bf16[64,32]{0,1:T(8,128)(2,1)S(1)}, bf16[64,32]{0,1:T(8,128)(2,1)}, u32[]{:S(2)}) copy-start(bf16[64,32]{0,1:T(8,128)(2,1)} %param.10) | copy-start | bytes 12292
  100.9 7.0 %copy-start.5 = (f32[128]{0:T(128)S(1)}, f32[128]{0:T(128)}, u32[]{:S(2)}) copy-start(f32[128]{0:T(128)} %param.13) | copy-start | bytes 1540
Sparse Core Ops, SparseCore 0:
  36.7 52.6 all-gather.1
where the time goes:
time: 117 us; the launch traced here: 116 us
  waiting for transfers between devices  51.1 us (44%)
  blocking collectives  21.7 us (19%)
  local copies, waits for them, and re-layouts  19.7 us (17%)
  between operations  13.6 us (12%)
  matrix products  5.84 us (5%)
  other arithmetic  4.31 us (4%)
    all_gather x1, waiting for transfers between devices, on_device(): lax.all_gather(right, 'res', axis=1, tiled=True)  51.1 us
    all_to_all x1, blocking collectives, on_device(): lax.all_to_all(stacked_sequence_embedding, 'res', split_axis=1, concat_ax...  21.7 us
    convert_element_type x2, local copies, waits for them, and re-layouts, pair_block(): flat.reshape(left_count * right_count, width * width).astype(jnp.bfloat16)  15 us
    dot_general x1, matrix products, pair_block(): lax.dot_general(left, piece, (((0,), (0,)), ((), ())), preferred_element_...  3.47 us
  transfers between devices with their start and end apart: 1, of which 1 were waited for; matrix products, arithmetic and copies ran while one was open for 1% of the time, Pallas kernels for 0%

commit v1 on v0

v1 whole, which is shorter than its diff:
```python
import functools

import jax
import jax.numpy as jnp
from jax import lax
from jax.experimental import pallas as pl
from jax.experimental.pallas import tpu as pltpu
from jax.sharding import PartitionSpec as P

F32 = jnp.float32
BF16 = jnp.bfloat16
LANES = 128
PARTS = 4


def dot(a, b):
    return jnp.dot(a, b, preferred_element_type=F32)


def kernel(
    n,
    x_ref,
    gain_ref,
    offset_ref,
    lhs_ref,
    rhs_ref,
    pair_ref,
    shift_ref,
    out_ref,
    norm_scr,
    turn_scr,
    pair_scr,
    pair_t,
    left_send,
    left_all,
    left_t,
    right_all,
    flat,
    mix,
    l_send,
    l_recv,
    ring_send,
    ring_recv,
    peer_send,
    peer_recv,
):
    rows = x_ref.shape[0]
    chans, width = lhs_ref.shape
    residues = x_ref.shape[1] // chans
    resid = residues // n
    tiles = x_ref.shape[1] // LANES
    per_tile = LANES // chans
    chips = n // 2
    me = lax.axis_index("res")
    core = lax.rem(me, 2)
    chip = me // 2

    col = lax.rem(chip, 2)
    place = (chip // 2) * (1 - 2 * col) + col * (chips - 1)

    def device_at(where):
        where = lax.rem(where + chips, chips)
        back = where // (chips // 2)
        return 2 * ((1 - back) * (2 * where) + back * (2 * (chips - 1 - where) + 1)) + core

    peer = me + 1 - 2 * core
    right_dev = device_at(place + 1)
    left_dev = device_at(place - 1)

    barrier = pltpu.get_barrier_semaphore()

    def greet(k, carry):
        pl.semaphore_signal(
            barrier,
            inc=1,
            device_id={"res": lax.rem(me + k, n)},
            device_id_type=pl.DeviceIdType.MESH,
        )
        return carry

    lax.fori_loop(1, n, greet, 0)

    def same(shape, down, across):
        r = lax.broadcasted_iota(jnp.int32, shape, 0) // down
        c = lax.broadcasted_iota(jnp.int32, shape, 1) // across
        return r == c

    lhs = lhs_ref[...].astype(F32)
    reps = LANES // width
    lhs_wide = jnp.concatenate([lhs] * reps, axis=1)
    lhs_wide = jnp.concatenate([lhs_wide] * reps, axis=0)
    lhs_wide = jnp.where(same(lhs_wide.shape, chans, width), lhs_wide, 0.0).astype(BF16)
    rhs = rhs_ref[...].astype(F32)
    rhs_wide = jnp.concatenate([rhs] * reps, axis=1)
    rhs_wide = jnp.concatenate([rhs_wide] * per_tile, axis=0)
    rhs_t = rhs_wide.T[:width, :].astype(BF16)
    averager = jnp.where(same((LANES, LANES), chans, chans), 1.0 / chans, 0.0).astype(BF16)
    gain = jnp.concatenate([gain_ref[...]] * per_tile, axis=1)
    offset = jnp.concatenate([offset_ref[...]] * per_tile, axis=1)

    group = 8
    dests = group * per_tile // resid
    halves = resid * width // LANES

    def project(b, carry):
        x = jnp.concatenate(
            [
                x_ref[:, pl.ds(pl.multiple_of((b * group + u) * LANES, LANES), LANES)].astype(F32)
                for u in range(group)
            ],
            axis=0,
        )
        center = x - dot(x.astype(BF16), averager)
        square = center * center
        high = square.astype(BF16)
        low = (square - high.astype(F32)).astype(BF16)
        spread = dot(high, averager) + dot(low, averager)
        normed = (center * lax.rsqrt(spread + 1e-05) * gain + offset).astype(BF16)
        wide = normed.astype(F32)
        norm_scr[pl.ds(pl.multiple_of(b * group * rows, 8), group * rows), :] = wide
        even = jnp.concatenate(
            [wide[u * rows : (u + 1) * rows] for u in range(0, group, 2)], axis=0
        ).astype(BF16)
        odd = jnp.concatenate(
            [wide[u * rows : (u + 1) * rows] for u in range(1, group, 2)], axis=0
        ).astype(BF16)
        left = dot(jnp.concatenate([even, odd], axis=1), lhs_wide)
        for u in range(group // 2):
            left_send[b * dests + u // halves, :, (u % halves) * LANES : (u % halves + 1) * LANES] = (
                left[u * rows : (u + 1) * rows].astype(BF16)
            )
        return carry

    lax.fori_loop(0, tiles // group, project, 0)

    lane = lax.broadcasted_iota(jnp.int32, (tiles, LANES), 1) // chans

    def turn(s, carry):
        one = norm_scr[pl.ds(s, tiles, stride=rows), :]
        spread_out = jnp.concatenate(
            [jnp.where(lane == r, one, 0.0) for r in range(per_tile)], axis=0
        ).astype(BF16)
        res = lax.dot_general(
            rhs_t, spread_out, (((1,), (1,)), ((), ())), preferred_element_type=F32
        )
        for j in range(residues // LANES):
            turn_scr[j, pl.ds(s, width, stride=rows), :] = res[:, j * LANES : (j + 1) * LANES]
        return carry

    lax.fori_loop(0, rows, turn, 0)
    for q in range(width):
        for j in range(residues // LANES):
            right_all[me, :, q * residues + j * LANES : q * residues + (j + 1) * LANES] = (
                turn_scr[j, q * rows : (q + 1) * rows, :].astype(BF16)
            )

    pl.semaphore_wait(barrier, n - 1)

    part = width * residues // PARTS

    def block(dev, h):
        return right_all.at[dev, :, pl.ds(h * part, part)]

    def ring(h, step, shift):
        sign = 1 - 2 * (h % 2)
        ref = block(device_at(place - sign * (step + shift)), h)
        return pltpu.make_async_remote_copy(
            src_ref=ref,
            dst_ref=ref,
            send_sem=ring_send.at[h, step],
            recv_sem=ring_recv.at[h, step],
            device_id={"res": right_dev if h % 2 == 0 else left_dev},
            device_id_type=pl.DeviceIdType.MESH,
        )

    def share(h, step, theirs):
        sign = 1 - 2 * (h % 2)
        source = device_at(place - sign * step)
        if theirs:
            source = source + 1 - 2 * core
        ref = block(source, h)
        return pltpu.make_async_remote_copy(
            src_ref=ref,
            dst_ref=ref,
            send_sem=peer_send.at[h, step],
            recv_sem=peer_recv.at[h, step],
            device_id={"res": peer},
            device_id_type=pl.DeviceIdType.MESH,
        )

    def left_copy(k):
        to = lax.rem(me + k, n)
        return pltpu.make_async_remote_copy(
            src_ref=left_send.at[to],
            dst_ref=left_all.at[me],
            send_sem=l_send.at[k],
            recv_sem=l_recv.at[k],
            device_id={"res": to},
            device_id_type=pl.DeviceIdType.MESH,
        )

    for h in range(PARTS):
        ring(h, 0, 0).start()
    for h in range(PARTS):
        share(h, 0, False).start()

    def send_left(k, carry):
        left_copy(k).start()
        return carry

    lax.fori_loop(1, n, send_left, 0)
    left_all[me] = left_send[me]

    pair_scr[...] = pair_ref[...].astype(F32)
    for b in range(width // reps):
        some = jnp.concatenate(
            [pair_scr[pl.ds(b * reps + u, width, stride=width), :] for u in range(reps)], axis=0
        )
        pair_t[:, b * LANES : (b + 1) * LANES] = some.T.astype(BF16)

    def hop(step, carry):
        for h in range(PARTS):
            ring(h, step - 1, 1).wait_recv()
            ring(h, step, 0).start()
            share(h, step, False).start()
        return carry

    lax.fori_loop(1, chips - 1, hop, 0)
    for h in range(PARTS):
        ring(h, chips - 2, 1).wait_recv()
        share(h, chips - 1, False).start()

    def left_in(k, carry):
        source = lax.rem(me - k + n, n)
        pltpu.make_async_remote_copy(
            src_ref=left_send.at[source],
            dst_ref=left_all.at[source],
            send_sem=l_send.at[k],
            recv_sem=l_recv.at[k],
            device_id={"res": source},
            device_id_type=pl.DeviceIdType.MESH,
        ).wait_recv()
        return carry

    lax.fori_loop(1, n, left_in, 0)
    left_t[...] = (
        left_all[...].astype(F32).reshape(n * rows, resid * width).T.astype(BF16)
    )

    def peer_in(step, carry):
        for h in range(PARTS):
            share(h, step, True).wait_recv()
        return carry

    lax.fori_loop(0, chips, peer_in, 0)

    qs = 4
    total = n * rows

    def outer(b, carry):
        here = right_all[:, :, pl.ds(pl.multiple_of(b * qs * residues, LANES), qs * residues)]
        if rows % 16:
            here = here.astype(F32)
        here = here.reshape(total, qs * residues).astype(BF16)
        product = (dot(left_t[...], here) * (1.0 / total)).astype(BF16)
        for u in range(qs):
            for i in range(resid):
                flat[
                    pl.ds(pl.multiple_of((b * qs + u) * width, width), width),
                    i * residues : (i + 1) * residues,
                ] = product[i * width : (i + 1) * width, u * residues : (u + 1) * residues]
        return carry

    lax.fori_loop(0, width // qs, outer, 0)

    for i in range(0, resid, 2):
        mapped = dot(pair_t[...], flat[:, i * residues : (i + 2) * residues])
        for u in range(2):
            turned = mapped[:, u * residues : (u + 1) * residues].T + shift_ref[...]
            for r in range(per_tile):
                mix[i + u, pl.ds(r, tiles, stride=per_tile), :] = turned[
                    r * tiles : (r + 1) * tiles
                ]
            out_ref[i + u] = mix[i + u].astype(BF16)

    def drain(step, carry):
        for h in range(PARTS):
            ring(h, step, 0).wait_send()
            share(h, step, False).wait_send()
        return carry

    lax.fori_loop(0, chips - 1, drain, 0)
    for h in range(PARTS):
        share(h, chips - 1, False).wait_send()

    def left_out(k, carry):
        left_copy(k).wait_send()
        return carry

    lax.fori_loop(1, n, left_out, 0)


def on_device(n, x, gain, offset, lhs, rhs, pair, shift):
    rows = x.shape[0]
    chans, width = lhs.shape
    residues = x.shape[1] // chans
    resid = residues // n
    tiles = x.shape[1] // LANES
    chips = n // 2
    depth = width * width
    out_chans = pair.shape[1]
    vmem = pl.BlockSpec(memory_space=pltpu.VMEM)
    return pl.pallas_call(
        functools.partial(kernel, n),
        out_shape=jax.ShapeDtypeStruct((resid, residues, out_chans), BF16),
        in_specs=[vmem] * 7,
        out_specs=vmem,
        scratch_shapes=[
            pltpu.VMEM((tiles * rows, LANES), F32),
            pltpu.VMEM((residues // LANES, width * rows, LANES), F32),
            pltpu.VMEM((depth, out_chans), F32),
            pltpu.VMEM((out_chans, depth), BF16),
            pltpu.VMEM((n, rows, resid * width), BF16),
            pltpu.VMEM((n, rows, resid * width), BF16),
            pltpu.VMEM((resid * width, n * rows), BF16),
            pltpu.VMEM((n, rows, width * residues), BF16),
            pltpu.VMEM((depth, resid * residues), BF16),
            pltpu.VMEM((resid, residues, out_chans), F32),
            pltpu.SemaphoreType.DMA((n,)),
            pltpu.SemaphoreType.DMA((n,)),
            pltpu.SemaphoreType.DMA((PARTS, chips)),
            pltpu.SemaphoreType.DMA((PARTS, chips)),
            pltpu.SemaphoreType.DMA((PARTS, chips)),
            pltpu.SemaphoreType.DMA((PARTS, chips)),
        ],
        compiler_params=pltpu.CompilerParams(
            collective_id=0, has_side_effects=True, vmem_limit_bytes=56 * 1024 * 1024
        ),
    )(x, gain.reshape(1, -1), offset.reshape(1, -1), lhs, rhs, pair, shift.reshape(1, -1))


def solution(mesh):
    in_specs = (P(("grp", "res"), None), P(), P(), P(), P(), P(), P())
    out_specs = P(("grp", "res"), None, None)
    return jax.shard_map(
        functools.partial(on_device, mesh.shape["res"]),
        mesh=mesh,
        in_specs=in_specs,
        out_specs=out_specs,
        check_vma=False,
    )
```

time: 117 us -> 55.1 us (0.47)
  waiting for transfers between devices: 51.1 us -> 0 us
  Pallas kernels: 0 us -> 50.6 us
  blocking collectives: 21.7 us -> 0 us
  local copies, waits for them, and re-layouts: 19.7 us -> 3.76 us
  between operations: 13.6 us -> 0.01 us
  matrix products: 5.84 us -> 0 us
  other arithmetic: 4.31 us -> 0 us
    all_gather x1 -> x0, waiting for transfers between devices: 51.1 us -> none  [on_device(): lax.all_gather(right, 'res', axis=1, tiled=True)]
    pallas_call x0 -> x1, Pallas kernels: none -> 50.6 us  [on_device(): pl.pallas_call(functools.partial(kernel, n), out_shape=jax.ShapeDtypeStru...]
    all_to_all x1 -> x0, blocking collectives: 21.7 us -> none  [on_device(): lax.all_to_all(stacked_sequence_embedding, 'res', split_axis=1, concat_ax...]
    convert_element_type x5 -> x0, local copies, waits for them, and re-layouts: 16.4 us -> none  [the longest x2 15 us: pair_block(): flat.reshape(left_count * right_count, width * width).astype(jnp.bfloat16)]
    dot_general x4 -> x0, matrix products: 5.84 us -> none  [the longest x1 3.47 us: pair_block(): lax.dot_general(left, piece, (((0,), (0,)), ((), ())), preferred_element_...]
    unnamed x12 -> x5, local copies, waits for them, and re-layouts: 0.03 us -> 3.76 us
    convert_element_type x2 -> x0, other arithmetic: 2.41 us -> none  [the longest x1 2.3 us: normalize(): return (center * lax.rsqrt(spread + 1e-05) * normalizer_multiplier + norm...]
    reshape x2 -> x0, local copies, waits for them, and re-layouts: 2.15 us -> none  [the longest x1 1.44 us: project_both(): right = jnp.dot(normed, rhs_projected_tensor, preferred_element_type=jnp....]
  transfers between devices with their start and end apart: 1 -> 0, of which waited for: 1 -> 0; matrix products, arithmetic and copies ran while one was open for 1% -> 0% of each run, Pallas kernels for 0% -> 0%
where the time goes in v1:
time: 55.1 us; the launch traced here: 54.4 us
  Pallas kernels  50.6 us (92%)
  local copies, waits for them, and re-layouts  3.76 us (7%)
    pallas_call x1, Pallas kernels, on_device(): pl.pallas_call(functools.partial(kernel, n), out_shape=jax.ShapeDtypeStru...  50.6 us
    unnamed x5, local copies, waits for them, and re-layouts  3.76 us

profile of v1, /device:TPU:0, one launch (start us, length us, event | category | flops | bytes accessed | tf_op | source)
XLA Modules:
  0.0 54.4 jit_solution(15438911202324855133)
XLA Ops:
  0.0 0.0 copy-start
  0.0 1.4 %copy.8.lhs_ref = bf16[64,32]{1,0:T(8,128)(2,1)} copy(bf16[64,32]{0,1:T(8,128)(2,1)} %param.10) | data formatting | bytes 8192 | tf_op args[3]
  1.4 0.0 copy-done
  1.4 0.7 %copy.9.rhs_ref = bf16[64,32]{1,0:T(8,128)(2,1)} copy(bf16[64,32]{0,1:T(8,128)(2,1)S(1)} %copy-done) | data formatting | bytes 8192 | tf_op args[4]
  2.1 50.6 %shard_map.73 = bf16[8,128,128]{2,1,0:T(8,128)(2,1)} custom-call(bf16[32,8192]{1,0:T(8,128)(2,1)} %x_ref.1, f32[1,64]{1,0:T(1,128)} %bitcast.3, f32[1,64]{1,0:T(1,128)} %bitcast.4, bf16[64,32]{1,0:T(8,128)(2,1)} %copy.8.lhs_ref, bf16[64,32]{1,0:T(8,128)(2,1)} %copy.9.rhs_ref, bf16[1024,128]{1,0:T(8,128)(2,1)} %pair_ref.1, f32[1,128]{1,0:T(1,128)} %bitcast.5), custom_call_target="tpu_custom_call" | custom-call | tf_op jit(solution)/shard_map/pallas_call | solution.py:313
  52.7 1.7 %copy.11 = bf16[8,128,128]{2,1,0:T(8,128)(2,1)} copy(bf16[8,128,128]{2,1,0:T(8,128)(2,1)} %shard_map.73) | data formatting | bytes 524288
Async XLA Ops:
  0.0 1.4 %copy-start = (bf16[64,32]{0,1:T(8,128)(2,1)S(1)}, bf16[64,32]{0,1:T(8,128)(2,1)}, u32[]{:S(2)}) copy-start(bf16[64,32]{0,1:T(8,128)(2,1)} %param.11) | copy-start | bytes 12292

commit v2 on v1

v2 whole, which is shorter than its diff:
```python
import functools

import jax
import jax.numpy as jnp
from jax import lax
from jax.experimental import pallas as pl
from jax.experimental.pallas import tpu as pltpu
from jax.sharding import PartitionSpec as P

F32 = jnp.float32
BF16 = jnp.bfloat16
LANES = 128
PARTS = 2


def dot(a, b):
    return jnp.dot(a, b, preferred_element_type=F32)


def kernel(
    n,
    x_ref,
    gain_ref,
    offset_ref,
    lhs_ref,
    rhs_ref,
    pair_ref,
    shift_ref,
    out_ref,
    norm_scr,
    turn_scr,
    pair_scr,
    pair_t,
    left_send,
    left_all,
    left_t,
    right_all,
    flat,
    mix,
    sum_send,
    sum_recv,
    l_send,
    l_recv,
    r_send,
    r_recv,
    peer_send,
    peer_recv,
    s_send,
    s_recv,
):
    rows = x_ref.shape[0]
    width, chans = lhs_ref.shape
    residues = x_ref.shape[1] // chans
    resid = residues // n
    tiles = x_ref.shape[1] // LANES
    per_tile = LANES // chans
    team = n // 2
    chips = team // 2
    me = lax.axis_index("res")
    half = me // team
    seat = lax.rem(me, team)
    core = lax.rem(seat, 2)
    chip = seat // 2
    base = half * team
    partner = (1 - half) * team + seat
    peer_seat = seat + 1 - 2 * core

    def to(dev):
        return dict(device_id={"res": dev}, device_id_type=pl.DeviceIdType.MESH)

    barrier = pltpu.get_barrier_semaphore()

    def greet(k, carry):
        pl.semaphore_signal(barrier, inc=1, **to(base + lax.rem(seat + k, team)))
        return carry

    lax.fori_loop(1, team, greet, 0)
    pl.semaphore_signal(barrier, inc=1, **to(partner))

    def same(shape, down, across):
        r = lax.broadcasted_iota(jnp.int32, shape, 0) // down
        c = lax.broadcasted_iota(jnp.int32, shape, 1) // across
        return r == c

    reps = LANES // width
    lhs = jnp.concatenate([lhs_ref[...].astype(F32)] * per_tile, axis=1)
    lhs = jnp.concatenate([lhs] * reps, axis=0).T
    lhs_wide = jnp.concatenate([lhs] * (reps // per_tile), axis=0)
    lhs_wide = jnp.where(same(lhs_wide.shape, chans, width), lhs_wide, 0.0).astype(BF16)
    rhs_t = jnp.concatenate([rhs_ref[...].astype(F32)] * per_tile, axis=1).astype(BF16)
    averager = jnp.where(same((LANES, LANES), chans, chans), 1.0 / chans, 0.0).astype(BF16)
    gain = jnp.concatenate([gain_ref[...]] * per_tile, axis=1)
    offset = jnp.concatenate([offset_ref[...]] * per_tile, axis=1)

    group = 8
    dests = group * per_tile // resid
    halves = resid * width // LANES

    def project(b, carry):
        x = jnp.concatenate(
            [
                x_ref[:, pl.ds(pl.multiple_of((b * group + u) * LANES, LANES), LANES)].astype(F32)
                for u in range(group)
            ],
            axis=0,
        )
        center = x - dot(x.astype(BF16), averager)
        square = center * center
        high = square.astype(BF16)
        low = (square - high.astype(F32)).astype(BF16)
        spread = dot(high, averager) + dot(low, averager)
        normed = (center * lax.rsqrt(spread + 1e-05) * gain + offset).astype(BF16)
        wide = normed.astype(F32)
        norm_scr[pl.ds(pl.multiple_of(b * group * rows, 8), group * rows), :] = wide
        even = jnp.concatenate(
            [wide[u * rows : (u + 1) * rows] for u in range(0, group, 2)], axis=0
        ).astype(BF16)
        odd = jnp.concatenate(
            [wide[u * rows : (u + 1) * rows] for u in range(1, group, 2)], axis=0
        ).astype(BF16)
        left = dot(jnp.concatenate([even, odd], axis=1), lhs_wide)
        for u in range(group // 2):
            dest = b * dests + u // halves
            left_send[
                lax.rem(dest, team), dest // team, :, (u % halves) * LANES : (u % halves + 1) * LANES
            ] = left[u * rows : (u + 1) * rows].astype(BF16)
        return carry

    lax.fori_loop(0, tiles // group, project, 0)

    lane = lax.broadcasted_iota(jnp.int32, (tiles, LANES), 1) // chans

    def turn(s, carry):
        one = norm_scr[pl.ds(s, tiles, stride=rows), :]
        spread_out = jnp.concatenate(
            [jnp.where(lane == r, one, 0.0) for r in range(per_tile)], axis=0
        ).astype(BF16)
        res = lax.dot_general(
            rhs_t, spread_out, (((1,), (1,)), ((), ())), preferred_element_type=F32
        )
        for j in range(residues // LANES):
            turn_scr[j, pl.ds(s, width, stride=rows), :] = res[:, j * LANES : (j + 1) * LANES]
        return carry

    lax.fori_loop(0, rows, turn, 0)
    for q in range(width):
        for j in range(residues // LANES):
            right_all[seat, :, q * residues + j * LANES : q * residues + (j + 1) * LANES] = (
                turn_scr[j, q * rows : (q + 1) * rows, :].astype(BF16)
            )

    pl.semaphore_wait(barrier, team)

    part = width * residues // PARTS

    def block(at, h):
        return right_all.at[at, :, pl.ds(h * part, part)]

    def right_copy(k, h, incoming):
        other = 2 * lax.rem(chip + k + chips, chips) + core
        ref = block(other if incoming else seat, h)
        slot = chips - k if incoming else k
        return pltpu.make_async_remote_copy(
            src_ref=ref,
            dst_ref=ref,
            send_sem=r_send.at[h, slot],
            recv_sem=r_recv.at[h, slot],
            **to(base + other),
        )

    def share(k, h, theirs):
        source = 2 * lax.rem(chip + k, chips) + (1 - core if theirs else core)
        ref = block(source, h)
        return pltpu.make_async_remote_copy(
            src_ref=ref,
            dst_ref=ref,
            send_sem=peer_send.at[h, k],
            recv_sem=peer_recv.at[h, k],
            **to(base + peer_seat),
        )

    def left_copy(k, incoming):
        slot = team - k if incoming else k
        other = lax.rem(seat + k, team)
        return pltpu.make_async_remote_copy(
            src_ref=left_send.at[other],
            dst_ref=left_all.at[other if incoming else seat],
            send_sem=l_send.at[slot],
            recv_sem=l_recv.at[slot],
            **to(base + other),
        )

    def over(first, last, act):
        def step(k, carry):
            act(k)
            return carry

        lax.fori_loop(first, last, step, 0)

    for h in range(PARTS):
        over(1, chips, lambda k: right_copy(k, h, False).start())
        share(0, h, False).start()
    over(1, team, lambda k: left_copy(k, False).start())
    left_all[seat] = left_send[seat]

    pair_scr[...] = pair_ref[...].astype(F32)
    for b in range(width // reps):
        some = jnp.concatenate(
            [pair_scr[pl.ds(b * reps + u, width, stride=width), :] for u in range(reps)], axis=0
        )
        pair_t[:, b * LANES : (b + 1) * LANES] = some.T.astype(BF16)

    for h in range(PARTS):

        def pass_on(k):
            right_copy(k, h, True).wait_recv()
            share(k, h, False).start()

        over(1, chips, pass_on)
    over(1, team, lambda k: left_copy(k, True).wait_recv())
    for b in range(2):
        left_t[b] = (
            left_all[:, b].astype(F32).reshape(team * rows, resid * width).T.astype(BF16)
        )
    for h in range(PARTS):
        over(0, chips, lambda k: share(k, h, True).wait_recv())

    qs = 4
    here_rows = team * rows
    total = n * rows

    def fill(which):
        def outer(b):
            here = right_all[:, :, pl.ds(pl.multiple_of(b * qs * residues, LANES), qs * residues)]
            if rows % 16:
                here = here.astype(F32)
            here = here.reshape(here_rows, qs * residues).astype(BF16)
            product = (dot(left_t[which], here) * (1.0 / total)).astype(BF16)
            for u in range(qs):
                for i in range(resid):
                    flat[
                        pl.ds(pl.multiple_of((b * qs + u) * width, width), width),
                        i * residues : (i + 1) * residues,
                    ] = product[i * width : (i + 1) * width, u * residues : (u + 1) * residues]

        over(0, width // qs, outer)

    def sums(b):
        return pltpu.make_async_remote_copy(
            src_ref=sum_send.at[b],
            dst_ref=sum_recv.at[b],
            send_sem=s_send.at[b],
            recv_sem=s_recv.at[b],
            **to(partner),
        )

    def mapped(b):
        return dot(pair_t[...], flat[:, b * 2 * residues : (b + 1) * 2 * residues])

    fill(1 - half)
    for b in range(resid // 2):
        sum_send[b] = mapped(b).astype(BF16)
        sums(b).start()
    fill(half)
    for b in range(resid // 2):
        mine = mapped(b)
        sums(b).wait_recv()
        mine = mine + sum_recv[b].astype(F32)
        for u in range(2):
            turned = mine[:, u * residues : (u + 1) * residues].T + shift_ref[...]
            for r in range(per_tile):
                mix[2 * b + u, pl.ds(r, tiles, stride=per_tile), :] = turned[
                    r * tiles : (r + 1) * tiles
                ]
            out_ref[2 * b + u] = mix[2 * b + u].astype(BF16)

    for h in range(PARTS):
        over(1, chips, lambda k: right_copy(k, h, False).wait_send())
        over(0, chips, lambda k: share(k, h, False).wait_send())
    over(1, team, lambda k: left_copy(k, False).wait_send())
    for b in range(resid // 2):
        sums(b).wait_send()


def on_device(n, x, gain, offset, lhs, rhs, pair, shift):
    rows = x.shape[0]
    chans, width = lhs.shape
    residues = x.shape[1] // chans
    resid = residues // n
    tiles = x.shape[1] // LANES
    team = n // 2
    chips = team // 2
    depth = width * width
    out_chans = pair.shape[1]
    vmem = pl.BlockSpec(memory_space=pltpu.VMEM)
    return pl.pallas_call(
        functools.partial(kernel, n),
        out_shape=jax.ShapeDtypeStruct((resid, residues, out_chans), BF16),
        in_specs=[vmem] * 7,
        out_specs=vmem,
        scratch_shapes=[
            pltpu.VMEM((tiles * rows, LANES), F32),
            pltpu.VMEM((residues // LANES, width * rows, LANES), F32),
            pltpu.VMEM((depth, out_chans), F32),
            pltpu.VMEM((out_chans, depth), BF16),
            pltpu.VMEM((team, 2, rows, resid * width), BF16),
            pltpu.VMEM((team, 2, rows, resid * width), BF16),
            pltpu.VMEM((2, resid * width, team * rows), BF16),
            pltpu.VMEM((team, rows, width * residues), BF16),
            pltpu.VMEM((depth, resid * residues), BF16),
            pltpu.VMEM((resid, residues, out_chans), F32),
            pltpu.VMEM((resid // 2, out_chans, 2 * residues), BF16),
            pltpu.VMEM((resid // 2, out_chans, 2 * residues), BF16),
            pltpu.SemaphoreType.DMA((team,)),
            pltpu.SemaphoreType.DMA((team,)),
            pltpu.SemaphoreType.DMA((PARTS, chips)),
            pltpu.SemaphoreType.DMA((PARTS, chips)),
            pltpu.SemaphoreType.DMA((PARTS, chips)),
            pltpu.SemaphoreType.DMA((PARTS, chips)),
            pltpu.SemaphoreType.DMA((resid // 2,)),
            pltpu.SemaphoreType.DMA((resid // 2,)),
        ],
        compiler_params=pltpu.CompilerParams(
            collective_id=0, has_side_effects=True, vmem_limit_bytes=56 * 1024 * 1024
        ),
    )(x, gain.reshape(1, -1), offset.reshape(1, -1), lhs.T, rhs.T, pair, shift.reshape(1, -1))


def solution(mesh):
    in_specs = (P(("grp", "res"), None), P(), P(), P(), P(), P(), P())
    out_specs = P(("grp", "res"), None, None)
    return jax.shard_map(
        functools.partial(on_device, mesh.shape["res"]),
        mesh=mesh,
        in_specs=in_specs,
        out_specs=out_specs,
        check_vma=False,
    )
```

time: 55.1 us -> 49.7 us (0.902); the launches traced: 54.4 us -> 49.5 us
  Pallas kernels: 50.6 us -> 47.8 us
  local copies, waits for them, and re-layouts: 3.76 us -> 1.67 us
    pallas_call x1, Pallas kernels: 50.6 us -> 47.8 us  [on_device(): pl.pallas_call(functools.partial(kernel, n), out_shape=jax.ShapeDtypeStru...]
    unnamed x5 -> x1, local copies, waits for them, and re-layouts: 3.76 us -> 1.67 us
where the time goes in v2:
time: 49.7 us; the launch traced here: 49.5 us
  Pallas kernels  47.8 us (96%)
  local copies, waits for them, and re-layouts  1.67 us (3%)
    pallas_call x1, Pallas kernels, on_device(): pl.pallas_call(functools.partial(kernel, n), out_shape=jax.ShapeDtypeStru...  47.8 us
    unnamed x1, local copies, waits for them, and re-layouts  1.67 us

profile of v2, /device:TPU:0, one launch (start us, length us, event | category | flops | bytes accessed | tf_op | source)
XLA Modules:
  0.0 49.5 jit_solution(14316996182159709184)
XLA Ops:
  0.0 47.8 %shard_map.73 = bf16[8,128,128]{2,1,0:T(8,128)(2,1)} custom-call(bf16[32,8192]{1,0:T(8,128)(2,1)} %x_ref.1, f32[1,64]{1,0:T(1,128)} %bitcast.7, f32[1,64]{1,0:T(1,128)} %bitcast.8, bf16[32,64]{1,0:T(8,128)(2,1)} %bitcast.5, bf16[32,64]{1,0:T(8,128)(2,1)} %bitcast.6, bf16[1024,128]{1,0:T(8,128)(2,1)} %pair_ref.1, f32[1,128]{1,0:T(1,128)} %bitcast.9), custom_call_target="tpu_custom_call" | custom-call | tf_op jit(solution)/shard_map/pallas_call | solution.py:296
  47.8 1.7 %copy.9 = bf16[8,128,128]{2,1,0:T(8,128)(2,1)} copy(bf16[8,128,128]{2,1,0:T(8,128)(2,1)} %shard_map.73) | data formatting | bytes 524288

commit v3 on v2

--- a/solution.py
+++ b/solution.py
@@ -10,7 +10,7 @@
 F32 = jnp.float32
 BF16 = jnp.bfloat16
 LANES = 128
-PARTS = 2
+WAVES = 2
 
 
 def dot(a, b):
@@ -37,6 +37,7 @@
     right_all,
     flat,
     mix,
+    kept,
     sum_send,
     sum_recv,
     l_send,
@@ -87,7 +88,9 @@
     lhs = jnp.concatenate([lhs] * reps, axis=0).T
     lhs_wide = jnp.concatenate([lhs] * (reps // per_tile), axis=0)
     lhs_wide = jnp.where(same(lhs_wide.shape, chans, width), lhs_wide, 0.0).astype(BF16)
-    rhs_t = jnp.concatenate([rhs_ref[...].astype(F32)] * per_tile, axis=1).astype(BF16)
+    fold = width // 2
+    rhs = rhs_ref[...].astype(F32)
+    rhs_t = jnp.concatenate([rhs[:fold], rhs[fold:]], axis=1).astype(BF16)
     averager = jnp.where(same((LANES, LANES), chans, chans), 1.0 / chans, 0.0).astype(BF16)
     gain = jnp.concatenate([gain_ref[...]] * per_tile, axis=1)
     offset = jnp.concatenate([offset_ref[...]] * per_tile, axis=1)
@@ -128,30 +131,9 @@
 
     lax.fori_loop(0, tiles // group, project, 0)
 
-    lane = lax.broadcasted_iota(jnp.int32, (tiles, LANES), 1) // chans
-
-    def turn(s, carry):
-        one = norm_scr[pl.ds(s, tiles, stride=rows), :]
-        spread_out = jnp.concatenate(
-            [jnp.where(lane == r, one, 0.0) for r in range(per_tile)], axis=0
-        ).astype(BF16)
-        res = lax.dot_general(
-            rhs_t, spread_out, (((1,), (1,)), ((), ())), preferred_element_type=F32
-        )
-        for j in range(residues // LANES):
-            turn_scr[j, pl.ds(s, width, stride=rows), :] = res[:, j * LANES : (j + 1) * LANES]
-        return carry
-
-    lax.fori_loop(0, rows, turn, 0)
-    for q in range(width):
-        for j in range(residues // LANES):
-            right_all[seat, :, q * residues + j * LANES : q * residues + (j + 1) * LANES] = (
-                turn_scr[j, q * rows : (q + 1) * rows, :].astype(BF16)
-            )
-
     pl.semaphore_wait(barrier, team)
 
-    part = width * residues // PARTS
+    part = width * residues // WAVES
 
     def block(at, h):
         return right_all.at[at, :, pl.ds(h * part, part)]
@@ -197,41 +179,79 @@
 
         lax.fori_loop(first, last, step, 0)
 
-    for h in range(PARTS):
+    over(1, team, lambda k: left_copy(k, False).start())
+
+    lane = lax.broadcasted_iota(jnp.int32, (tiles, LANES), 1) // chans
+    strips = residues // LANES
+
+    def turn(s):
+        one = norm_scr[pl.ds(s, tiles, stride=rows), :]
+        swapped = pltpu.roll(one, chans, 1)
+        spread_out = jnp.concatenate(
+            [
+                jnp.where(lane == q, one if q == r else swapped, 0.0)
+                for r in range(2)
+                for q in range(2)
+            ],
+            axis=0,
+        ).astype(BF16)
+        res = lax.dot_general(
+            rhs_t, spread_out, (((1,), (1,)), ((), ())), preferred_element_type=F32
+        )
+        for j in range(2 * strips):
+            turn_scr[j, pl.ds(s, fold, stride=rows), :] = res[:, j * LANES : (j + 1) * LANES]
+
+    over(0, rows, turn)
+    for h in range(WAVES):
+        for q in range(fold):
+            for j in range(strips):
+                at = (h * fold + q) * residues + j * LANES
+                right_all[seat, :, at : at + LANES] = turn_scr[
+                    h * strips + j, q * rows : (q + 1) * rows, :
+                ].astype(BF16)
         over(1, chips, lambda k: right_copy(k, h, False).start())
         share(0, h, False).start()
-    over(1, team, lambda k: left_copy(k, False).start())
     left_all[seat] = left_send[seat]
 
+    out_chans = pair_ref.shape[1]
     pair_scr[...] = pair_ref[...].astype(F32)
-    for b in range(width // reps):
-        some = jnp.concatenate(
-            [pair_scr[pl.ds(b * reps + u, width, stride=width), :] for u in range(reps)], axis=0
-        )
-        pair_t[:, b * LANES : (b + 1) * LANES] = some.T.astype(BF16)
-
-    for h in range(PARTS):
-
+    for c in range(2):
+        for b in range(fold // reps):
+            some = jnp.concatenate(
+                [
+                    pair_scr[pl.ds(c * fold + b * reps + u, width, stride=width), :]
+                    for u in range(reps)
+                ],
+                axis=0,
+            )
+            pair_t[c * out_chans : (c + 1) * out_chans, b * LANES : (b + 1) * LANES] = (
+                some.T.astype(BF16)
+            )
+
+    def gather(h):
         def pass_on(k):
             right_copy(k, h, True).wait_recv()
             share(k, h, False).start()
 
         over(1, chips, pass_on)
-    over(1, team, lambda k: left_copy(k, True).wait_recv())
-    for b in range(2):
-        left_t[b] = (
-            left_all[:, b].astype(F32).reshape(team * rows, resid * width).T.astype(BF16)
-        )
-    for h in range(PARTS):
+
+    def gathered(h):
         over(0, chips, lambda k: share(k, h, True).wait_recv())
 
     qs = 4
     here_rows = team * rows
     total = n * rows
-
-    def fill(which):
+    first = lax.broadcasted_iota(jnp.int32, (out_chans, residues), 1) < tiles
+
+    def fill(which, h):
         def outer(b):
-            here = right_all[:, :, pl.ds(pl.multiple_of(b * qs * residues, LANES), qs * residues)]
+            here = right_all[
+                :,
+                :,
+                pl.ds(
+                    pl.multiple_of(h * fold * residues + b * qs * residues, LANES), qs * residues
+                ),
+            ]
             if rows % 16:
                 here = here.astype(F32)
             here = here.reshape(here_rows, qs * residues).astype(BF16)
@@ -243,43 +263,67 @@
                         i * residues : (i + 1) * residues,
                     ] = product[i * width : (i + 1) * width, u * residues : (u + 1) * residues]
 
-        over(0, width // qs, outer)
-
-    def sums(b):
+        over(0, fold // qs, outer)
+
+    def sums(b, h):
         return pltpu.make_async_remote_copy(
-            src_ref=sum_send.at[b],
-            dst_ref=sum_recv.at[b],
-            send_sem=s_send.at[b],
-            recv_sem=s_recv.at[b],
+            src_ref=sum_send.at[h, b],
+            dst_ref=sum_recv.at[h, b],
+            send_sem=s_send.at[h, b],
+            recv_sem=s_recv.at[h, b],
             **to(partner),
         )
 
     def mapped(b):
-        return dot(pair_t[...], flat[:, b * 2 * residues : (b + 1) * 2 * residues])
-
-    fill(1 - half)
-    for b in range(resid // 2):
-        sum_send[b] = mapped(b).astype(BF16)
-        sums(b).start()
-    fill(half)
-    for b in range(resid // 2):
-        mine = mapped(b)
-        sums(b).wait_recv()
-        mine = mine + sum_recv[b].astype(F32)
-        for u in range(2):
-            turned = mine[:, u * residues : (u + 1) * residues].T + shift_ref[...]
-            for r in range(per_tile):
-                mix[2 * b + u, pl.ds(r, tiles, stride=per_tile), :] = turned[
-                    r * tiles : (r + 1) * tiles
-                ]
-            out_ref[2 * b + u] = mix[2 * b + u].astype(BF16)
-
-    for h in range(PARTS):
+        both = dot(pair_t[...], flat[:, b * 2 * residues : (b + 1) * 2 * residues])
+        low, high = both[:out_chans], both[out_chans:]
+        one = low[:, :residues] + pltpu.roll(high[:, :residues], tiles, 1)
+        two = pltpu.roll(low[:, residues:], tiles, 1) + high[:, residues:]
+        return jnp.where(first, one, two)
+
+    def theirs(h):
+        fill(1 - half, h)
+        for b in range(resid // 2):
+            sum_send[h, b] = mapped(b).astype(BF16)
+            sums(b, h).start()
+
+    def mine(h):
+        fill(half, h)
+        for b in range(resid // 2):
+            kept[h, b] = mapped(b)
+
+    def finish(h):
+        for b in range(resid // 2):
+            sums(b, h).wait_recv()
+            turned = (kept[h, b] + sum_recv[h, b].astype(F32)).T + shift_ref[...]
+            for u in range(2):
+                mix[2 * b + u, pl.ds(h, tiles, stride=2), :] = turned[u * tiles : (u + 1) * tiles]
+
+    gather(0)
+    over(1, team, lambda k: left_copy(k, True).wait_recv())
+    for b in range(2):
+        left_t[b] = (
+            left_all[:, b].astype(F32).reshape(team * rows, resid * width).T.astype(BF16)
+        )
+    gathered(0)
+    theirs(0)
+    gather(1)
+    mine(0)
+    gathered(1)
+    theirs(1)
+    mine(1)
+    finish(0)
+    finish(1)
+    for i in range(resid):
+        out_ref[i] = mix[i].astype(BF16)
+
+    for h in range(WAVES):
         over(1, chips, lambda k: right_copy(k, h, False).wait_send())
         over(0, chips, lambda k: share(k, h, False).wait_send())
     over(1, team, lambda k: left_copy(k, False).wait_send())
-    for b in range(resid // 2):
-        sums(b).wait_send()
+    for h in range(WAVES):
+        for b in range(resid // 2):
+            sums(b, h).wait_send()
 
 
 def on_device(n, x, gain, offset, lhs, rhs, pair, shift):
@@ -300,25 +344,26 @@
         out_specs=vmem,
         scratch_shapes=[
             pltpu.VMEM((tiles * rows, LANES), F32),
-            pltpu.VMEM((residues // LANES, width * rows, LANES), F32),
+            pltpu.VMEM((2 * residues // LANES, width // 2 * rows, LANES), F32),
             pltpu.VMEM((depth, out_chans), F32),
-            pltpu.VMEM((out_chans, depth), BF16),
+            pltpu.VMEM((2 * out_chans, depth // 2), BF16),
             pltpu.VMEM((team, 2, rows, resid * width), BF16),
             pltpu.VMEM((team, 2, rows, resid * width), BF16),
             pltpu.VMEM((2, resid * width, team * rows), BF16),
             pltpu.VMEM((team, rows, width * residues), BF16),
-            pltpu.VMEM((depth, resid * residues), BF16),
+            pltpu.VMEM((depth // 2, resid * residues), BF16),
             pltpu.VMEM((resid, residues, out_chans), F32),
-            pltpu.VMEM((resid // 2, out_chans, 2 * residues), BF16),
-            pltpu.VMEM((resid // 2, out_chans, 2 * residues), BF16),
+            pltpu.VMEM((WAVES, resid // 2, out_chans, residues), F32),
+            pltpu.VMEM((WAVES, resid // 2, out_chans, residues), BF16),
+            pltpu.VMEM((WAVES, resid // 2, out_chans, residues), BF16),
             pltpu.SemaphoreType.DMA((team,)),
             pltpu.SemaphoreType.DMA((team,)),
-            pltpu.SemaphoreType.DMA((PARTS, chips)),
-            pltpu.SemaphoreType.DMA((PARTS, chips)),
-            pltpu.SemaphoreType.DMA((PARTS, chips)),
-            pltpu.SemaphoreType.DMA((PARTS, chips)),
-            pltpu.SemaphoreType.DMA((resid // 2,)),
-            pltpu.SemaphoreType.DMA((resid // 2,)),
+            pltpu.SemaphoreType.DMA((WAVES, chips)),
+            pltpu.SemaphoreType.DMA((WAVES, chips)),
+            pltpu.SemaphoreType.DMA((WAVES, chips)),
+            pltpu.SemaphoreType.DMA((WAVES, chips)),
+            pltpu.SemaphoreType.DMA((WAVES, resid // 2)),
+            pltpu.SemaphoreType.DMA((WAVES, resid // 2)),
         ],
         compiler_params=pltpu.CompilerParams(
             collective_id=0, has_side_effects=True, vmem_limit_bytes=56 * 1024 * 1024

time: 49.7 us -> 44.4 us (0.89)
  Pallas kernels: 47.8 us -> 42.6 us
    pallas_call x1, Pallas kernels: 47.8 us -> 42.6 us  [on_device(): pl.pallas_call(functools.partial(kernel, n), out_shape=jax.ShapeDtypeStru...]
where the time goes in v3:
time: 44.4 us; the launch traced here: 44.3 us
  Pallas kernels  42.6 us (96%)
  local copies, waits for them, and re-layouts  1.67 us (4%)
    pallas_call x1, Pallas kernels, on_device(): pl.pallas_call(functools.partial(kernel, n), out_shape=jax.ShapeDtypeStru...  42.6 us
    unnamed x1, local copies, waits for them, and re-layouts  1.67 us

profile of v3, /device:TPU:0, one launch (start us, length us, event | category | flops | bytes accessed | tf_op | source)
XLA Modules:
  0.0 44.3 jit_solution(17609819402390788792)
XLA Ops:
  0.0 42.6 %shard_map.73 = bf16[8,128,128]{2,1,0:T(8,128)(2,1)} custom-call(bf16[32,8192]{1,0:T(8,128)(2,1)} %x_ref.1, f32[1,64]{1,0:T(1,128)} %bitcast.7, f32[1,64]{1,0:T(1,128)} %bitcast.8, bf16[32,64]{1,0:T(8,128)(2,1)} %bitcast.5, bf16[32,64]{1,0:T(8,128)(2,1)} %bitcast.6, bf16[1024,128]{1,0:T(8,128)(2,1)} %pair_ref.1, f32[1,128]{1,0:T(1,128)} %bitcast.9), custom_call_target="tpu_custom_call" | custom-call | tf_op jit(solution)/shard_map/pallas_call | solution.py:340
  42.6 1.7 %copy.9 = bf16[8,128,128]{2,1,0:T(8,128)(2,1)} copy(bf16[8,128,128]{2,1,0:T(8,128)(2,1)} %shard_map.73) | data formatting | bytes 524288

commit v4 on v3

--- a/solution.py
+++ b/solution.py
@@ -184,13 +184,14 @@
     lane = lax.broadcasted_iota(jnp.int32, (tiles, LANES), 1) // chans
     strips = residues // LANES
 
-    def turn(s):
-        one = norm_scr[pl.ds(s, tiles, stride=rows), :]
-        swapped = pltpu.roll(one, chans, 1)
+    batch = 8
+
+    def turn(b, h):
+        ones = [norm_scr[pl.ds(b * batch + v, tiles, stride=rows), :] for v in range(batch)]
         spread_out = jnp.concatenate(
             [
-                jnp.where(lane == q, one if q == r else swapped, 0.0)
-                for r in range(2)
+                jnp.where(lane == q, one if q == h else pltpu.roll(one, chans, 1), 0.0)
+                for one in ones
                 for q in range(2)
             ],
             axis=0,
@@ -198,11 +199,15 @@
         res = lax.dot_general(
             rhs_t, spread_out, (((1,), (1,)), ((), ())), preferred_element_type=F32
         )
-        for j in range(2 * strips):
-            turn_scr[j, pl.ds(s, fold, stride=rows), :] = res[:, j * LANES : (j + 1) * LANES]
-
-    over(0, rows, turn)
+        for v in range(batch):
+            for j in range(strips):
+                at = v * residues + j * LANES
+                turn_scr[h * strips + j, pl.ds(b * batch + v, fold, stride=rows), :] = res[
+                    :, at : at + LANES
+                ]
+
     for h in range(WAVES):
+        over(0, rows // batch, lambda b: turn(b, h))
         for q in range(fold):
             for j in range(strips):
                 at = (h * fold + q) * residues + j * LANES

time: 44.4 us -> 38.7 us (0.87)
  Pallas kernels: 42.6 us -> 36.9 us
    pallas_call x1, Pallas kernels: 42.6 us -> 36.9 us  [on_device(): pl.pallas_call(functools.partial(kernel, n), out_shape=jax.ShapeDtypeStru...]
where the time goes in v4:
time: 38.7 us; the launch traced here: 38.6 us
  Pallas kernels  36.9 us (95%)
  local copies, waits for them, and re-layouts  1.67 us (4%)
    pallas_call x1, Pallas kernels, on_device(): pl.pallas_call(functools.partial(kernel, n), out_shape=jax.ShapeDtypeStru...  36.9 us
    unnamed x1, local copies, waits for them, and re-layouts  1.67 us

profile of v4, /device:TPU:0, one launch (start us, length us, event | category | flops | bytes accessed | tf_op | source)
XLA Modules:
  0.0 38.6 jit_solution(11906965272564613916)
XLA Ops:
  0.0 36.9 %shard_map.73 = bf16[8,128,128]{2,1,0:T(8,128)(2,1)} custom-call(bf16[32,8192]{1,0:T(8,128)(2,1)} %x_ref.1, f32[1,64]{1,0:T(1,128)} %bitcast.7, f32[1,64]{1,0:T(1,128)} %bitcast.8, bf16[32,64]{1,0:T(8,128)(2,1)} %bitcast.5, bf16[32,64]{1,0:T(8,128)(2,1)} %bitcast.6, bf16[1024,128]{1,0:T(8,128)(2,1)} %pair_ref.1, f32[1,128]{1,0:T(1,128)} %bitcast.9), custom_call_target="tpu_custom_call" | custom-call | tf_op jit(solution)/shard_map/pallas_call | solution.py:345
  36.9 1.7 %copy.9 = bf16[8,128,128]{2,1,0:T(8,128)(2,1)} copy(bf16[8,128,128]{2,1,0:T(8,128)(2,1)} %shard_map.73) | data formatting | bytes 524288

commit v5 on v4

--- a/solution.py
+++ b/solution.py
@@ -268,7 +268,8 @@
                         i * residues : (i + 1) * residues,
                     ] = product[i * width : (i + 1) * width, u * residues : (u + 1) * residues]
 
-        over(0, fold // qs, outer)
+        for b in range(fold // qs):
+            outer(b)
 
     def sums(b, h):
         return pltpu.make_async_remote_copy(

time: 38.7 us -> 37.8 us (0.977)
  Pallas kernels: 36.9 us -> 35.9 us
    pallas_call x1, Pallas kernels: 36.9 us -> 35.9 us  [on_device(): pl.pallas_call(functools.partial(kernel, n), out_shape=jax.ShapeDtypeStru...]
where the time goes in v5:
time: 37.8 us; the launch traced here: 37.6 us
  Pallas kernels  35.9 us (95%)
  local copies, waits for them, and re-layouts  1.67 us (4%)
    pallas_call x1, Pallas kernels, on_device(): pl.pallas_call(functools.partial(kernel, n), out_shape=jax.ShapeDtypeStru...  35.9 us
    unnamed x1, local copies, waits for them, and re-layouts  1.67 us

profile of v5, /device:TPU:0, one launch (start us, length us, event | category | flops | bytes accessed | tf_op | source)
XLA Modules:
  0.0 37.6 jit_solution(14423277569051772233)
XLA Ops:
  0.0 35.9 %shard_map.73 = bf16[8,128,128]{2,1,0:T(8,128)(2,1)} custom-call(bf16[32,8192]{1,0:T(8,128)(2,1)} %x_ref.1, f32[1,64]{1,0:T(1,128)} %bitcast.7, f32[1,64]{1,0:T(1,128)} %bitcast.8, bf16[32,64]{1,0:T(8,128)(2,1)} %bitcast.5, bf16[32,64]{1,0:T(8,128)(2,1)} %bitcast.6, bf16[1024,128]{1,0:T(8,128)(2,1)} %pair_ref.1, f32[1,128]{1,0:T(1,128)} %bitcast.9), custom_call_target="tpu_custom_call" | custom-call | tf_op jit(solution)/shard_map/pallas_call | solution.py:346
  35.9 1.7 %copy.9 = bf16[8,128,128]{2,1,0:T(8,128)(2,1)} copy(bf16[8,128,128]{2,1,0:T(8,128)(2,1)} %shard_map.73) | data formatting | bytes 524288
